TPU v7x, 32 devices: a whole 2x2x4 slice. The times are simulated.
32 devices in a mesh: vp: 4 (over y, x), cp: 2 (over core), ga: 4 (over z).
Axes of the slice: x: 2, y: 2, z: 4, core: 2. Of those that a mesh axis runs over, the one named last changes fastest.
Arguments:
- valence_wavefunction: bfloat16 [512, 24576], P(('vp', 'cp'), 'ga'), may hold values from -6 to 6
- cond_wave: bfloat16 [512, 24576], P(('vp', 'cp'), 'ga'), may hold values from -6 to 6
- screen_basis: bfloat16 [24576, 1024], P('ga'), may hold values from -0.0390625 to 0.0390625
- screen: float32 [1024], replicated, may hold values from 0.01 to 0.1
- coulomb: float32 [1024], replicated, may hold values from 0.02 to 0.2
- window_rows: int32 [2], replicated, may hold values from 0 to 1023
- tile_owner: int32 [48], P(('vp', 'cp')), may hold values from 0 to 4095, as said below
Outputs:
- kernel: float32 [2, 48, 4096], P(None, ('vp', 'cp'), 'ga')
Inputs may be any that keep to these rules, and one draw needn't show every extreme that they name: `tile_owner`: distinct pair-block indices; 0 and 4095 both occur.
All inputs are finite; a program needn't handle non-finite values.
Results may differ from a plain program's by a relative error of at most 0.02.
Values may be sent and summed in bfloat16 or wider, within the bound.
A program may use at most 64 MiB of HBM per device.

v0:
```python
import jax
import jax.numpy as jnp
from jax import lax
from jax.sharding import PartitionSpec as P

R = 1024
TV = 8
TC = 8
NCT = 64


def select_bands(wanted, shard_part):
    row_ids = jnp.arange(shard_part.shape[0], dtype=jnp.int32)
    chooser = (wanted[:, None] == row_ids[None, :]).astype(jnp.bfloat16)
    return jnp.dot(chooser, shard_part, preferred_element_type=jnp.float32)


def outer_rows(left_wavefunction, right_wave):
    product = (
        left_wavefunction.astype(jnp.float32)[..., :, None, :]
        * right_wave.astype(jnp.float32)[..., None, :, :]
    )
    return product.astype(jnp.bfloat16)


def contract(row_proj, col_proj, val_proj, cond_proj, screen_part, coulomb_part):
    exchange_term = jnp.einsum(
        "qacr,svdr->qsacvd", row_proj * coulomb_part, col_proj, precision=lax.Precision.HIGHEST
    )
    direct_term = jnp.einsum(
        "qsavr,qscdr->qsacvd", val_proj * screen_part, cond_proj, precision=lax.Precision.HIGHEST
    )
    total = 2.0 * exchange_term - direct_term
    return total.reshape(total.shape[0], total.shape[1], -1)


def shards(valence_wavefunction, cond_wave, screen_basis, screen, coulomb, window_rows, tile_owner):
    slot_count = tile_owner.shape[0]
    grid_count = valence_wavefunction.shape[1]
    pair_tiles = jnp.concatenate([window_rows, tile_owner])
    val_wanted = (
        (pair_tiles // NCT)[:, None] * TV + jnp.arange(TV, dtype=jnp.int32)[None, :]
    ).reshape(-1)
    conduction_wanted = (
        (pair_tiles % NCT)[:, None] * TC + jnp.arange(TC, dtype=jnp.int32)[None, :]
    ).reshape(-1)
    picked_val = select_bands(
        val_wanted, lax.all_gather(valence_wavefunction, ("vp", "cp"), axis=0, tiled=True)
    )
    picked_cond = select_bands(
        conduction_wanted, lax.all_gather(cond_wave, ("vp", "cp"), axis=0, tiled=True)
    )
    picked_val = picked_val.astype(jnp.bfloat16).reshape(2 + slot_count, TV, grid_count)
    picked_cond = picked_cond.astype(jnp.bfloat16).reshape(2 + slot_count, TC, grid_count)
    row_val = picked_val[:2]
    slot_valence = picked_val[2:]
    row_cond = picked_cond[:2]
    slot_cond = picked_cond[2:]
    row_rho = outer_rows(row_val, row_cond).reshape(2 * TV * TC, grid_count)
    col_rho = outer_rows(slot_valence, slot_cond).reshape(slot_count * TV * TC, grid_count)
    val_rho = outer_rows(row_val[:, None], slot_valence[None]).reshape(
        2 * slot_count * TV * TV, grid_count
    )
    cond_rho = outer_rows(row_cond[:, None], slot_cond[None]).reshape(
        2 * slot_count * TC * TC, grid_count
    )
    row_part = jnp.dot(row_rho, screen_basis, preferred_element_type=jnp.float32)
    col_part = jnp.dot(col_rho, screen_basis, preferred_element_type=jnp.float32)
    val_part = jnp.dot(val_rho, screen_basis, preferred_element_type=jnp.float32)
    cond_part = jnp.dot(cond_rho, screen_basis, preferred_element_type=jnp.float32)
    live_tile = (tile_owner[None, :] >= window_rows[:, None])[:, :, None]
    grid_groups = lax.axis_size("ga")
    rank_span = R // grid_groups
    rank_first = lax.axis_index("ga") * rank_span
    row_sum, col_sum, val_sum, cond_sum = (
        lax.psum_scatter(
            row_part.astype(jnp.bfloat16), "ga", scatter_dimension=1, tiled=True
        ).astype(jnp.float32),
        lax.psum_scatter(
            col_part.astype(jnp.bfloat16), "ga", scatter_dimension=1, tiled=True
        ).astype(jnp.float32),
        lax.psum_scatter(
            val_part.astype(jnp.bfloat16), "ga", scatter_dimension=1, tiled=True
        ).astype(jnp.float32),
        lax.psum_scatter(
            cond_part.astype(jnp.bfloat16), "ga", scatter_dimension=1, tiled=True
        ).astype(jnp.float32),
    )
    screen_part = lax.dynamic_slice_in_dim(screen, rank_first, rank_span, 0)
    coulomb_part = lax.dynamic_slice_in_dim(coulomb, rank_first, rank_span, 0)
    kernel = contract(
        row_sum.reshape(2, TV, TC, rank_span),
        col_sum.reshape(slot_count, TV, TC, rank_span),
        val_sum.reshape(2, slot_count, TV, TV, rank_span),
        cond_sum.reshape(2, slot_count, TC, TC, rank_span),
        screen_part,
        coulomb_part,
    )
    kernel = jnp.where(live_tile, kernel, jnp.zeros_like(kernel))
    return lax.psum_scatter(
        kernel.astype(jnp.bfloat16), "ga", scatter_dimension=2, tiled=True
    ).astype(jnp.float32)


def solution(mesh):
    in_specs = (
        P(("vp", "cp"), "ga"),
        P(("vp", "cp"), "ga"),
        P("ga", None),
        P(),
        P(),
        P(),
        P(("vp", "cp")),
    )
    out_specs = P(None, ("vp", "cp"), "ga")
    return jax.shard_map(shards, mesh=mesh, in_specs=in_specs, out_specs=out_specs, check_vma=False)
```

profile of v0, /device:TPU:0, one launch (start us, length us, event | category | flops | bytes accessed | tf_op | source)
XLA Modules:
  0.0 302.0 jit_solution(14764287237343330676)
XLA Ops:
  6.5 0.7 all-gather.3.cloned.1.call-update
  7.3 0.7 all-gather.5.cloned.1.call-update
  8.1 0.8 fusion.10
  9.1 48.2 %all-gather.3.cloned.1.call-done = bf16[512,6144]{1,0:T(8,128)(2,1)} async-done(((bf16[64,6144]{1,0:T(8,128)(2,1)}), bf16[512,6144]{1,0:T(8,128)(2,1)}) %all-gather.3.cloned.1.call-update) | async-done | bytes 6291472 | tf_op jit(solution)/shard_map/all_gather | solution.py:48
  57.4 4.0 %convolution_convert_fusion.1 = bf16[64,6144]{1,0:T(8,128)(2,1)S(1)} fusion(bf16[512,6144]{1,0:T(8,128)(2,1)} %all-gather.3.cloned.1.call-done, s32[64]{0:T(128)S(1)} %add.72), kind=kOutput, calls=%fused_computation.4 | convolution fusion | flops 403079168 | bytes 7078144 | tf_op jit(solution)/shard_map/dot_general | solution.py:15
  61.5 43.1 %all-gather.5.cloned.1.call-done = bf16[512,6144]{1,0:T(8,128)(2,1)} async-done(((bf16[64,6144]{1,0:T(8,128)(2,1)}), bf16[512,6144]{1,0:T(8,128)(2,1)}) %all-gather.5.cloned.1.call-update) | async-done | bytes 6291472 | tf_op jit(solution)/shard_map/all_gather | solution.py:51
  104.7 4.0 %convolution_convert_fusion = bf16[64,6144]{1,0:T(8,128)(2,1)S(1)} fusion(bf16[512,6144]{1,0:T(8,128)(2,1)} %all-gather.5.cloned.1.call-done, s32[64]{0:T(128)S(1)} %add.77), kind=kOutput, calls=%fused_computation.3 | convolution fusion | flops 403079168 | bytes 7078144 | tf_op jit(solution)/shard_map/dot_general | solution.py:15
  109.1 7.1 %convolution_convert_fusion.5 = bf16[128,1024]{1,0:T(8,128)(2,1)} fusion(bf16[128,6144]{1,0:T(8,128)(2,1)S(1)} %bitcast.71, bf16[6144,1024]{1,0:T(8,128)(2,1)} %param.9), kind=kOutput, calls=%fused_computation.10 | convolution fusion | flops 1610743808 | bytes 14417920 | tf_op jit(solution)/shard_map/dot_general | solution.py:67
  116.2 5.7 %multiply_convert_fusion = bf16[2,6,8,8,6144]{4,3,2,1,0:T(8,128)(2,1)} fusion(f32[6,8,6144]{2,1,0:T(8,128)S(1)} %fusion.3, f32[2,8,6144]{2,1,0:T(8,128)S(1)} %fusion.6), kind=kLoop, calls=%fused_computation | loop fusion | flops 9437184 | bytes 11010048 | tf_op jit(solution)/shard_map/convert_element_type | solution.py:23
  121.9 15.7 %convolution_convert_fusion.2 = bf16[768,1024]{1,0:T(8,128)(2,1)} fusion(bf16[768,6144]{1,0:T(8,128)(2,1)} %bitcast.73, bf16[6144,1024]{1,0:T(8,128)(2,1)} %param.9), kind=kOutput, calls=%fused_computation.7 | convolution fusion | flops 9664462848 | bytes 23592960 | tf_op jit(solution)/shard_map/dot_general | solution.py:69
  137.6 5.7 %multiply_convert_fusion.1 = bf16[2,6,8,8,6144]{4,3,2,1,0:T(8,128)(2,1)} fusion(f32[6,8,6144]{2,1,0:T(8,128)S(1)} %fusion.2, f32[2,8,6144]{2,1,0:T(8,128)S(1)} %fusion.5), kind=kLoop, calls=%fused_computation.1 | loop fusion | flops 9437184 | bytes 11010048 | tf_op jit(solution)/shard_map/convert_element_type | solution.py:23
  143.5 15.7 %convolution_convert_fusion.3 = bf16[768,1024]{1,0:T(8,128)(2,1)} fusion(bf16[768,6144]{1,0:T(8,128)(2,1)} %bitcast.72, bf16[6144,1024]{1,0:T(8,128)(2,1)} %param.9), kind=kOutput, calls=%fused_computation.8 | convolution fusion | flops 9664462848 | bytes 23592960 | tf_op jit(solution)/shard_map/dot_general | solution.py:70
  159.3 0.8 multiply_convert_fusion.2
  160.2 9.1 %convolution_convert_fusion.4 = bf16[384,1024]{1,0:T(8,128)(2,1)} fusion(bf16[384,6144]{1,0:T(8,128)(2,1)S(1)} %bitcast.75, bf16[6144,1024]{1,0:T(8,128)(2,1)} %param.9), kind=kOutput, calls=%fused_computation.9 | convolution fusion | flops 4832231424 | bytes 18087936 | tf_op jit(solution)/shard_map/dot_general | solution.py:68
  169.3 0.3 reduce-scatter.16.cloned.1.call-start
  169.6 0.8 dynamic_slice.7
  170.3 0.8 dynamic_slice.6
  171.2 0.9 convert_multiply_fusion.2
  172.0 6.9 %reduce-scatter.14.cloned.1.call-done = bf16[768,256]{1,0:T(8,128)(2,1)} async-done(((bf16[768,1024]{1,0:T(8,128)(2,1)}), bf16[768,256]{1,0:T(8,128)(2,1)}) %reduce-scatter.14.cloned.1.call-update) | async-done | bytes 393232 | tf_op jit(solution)/shard_map/reduce_scatter | solution.py:82
  178.9 36.5 %reduce-scatter.12.cloned.1.call-done = bf16[768,256]{1,0:T(8,128)(2,1)} async-done(((bf16[768,1024]{1,0:T(8,128)(2,1)}), bf16[768,256]{1,0:T(8,128)(2,1)}) %reduce-scatter.12.cloned.1.call-update) | async-done | bytes 393232 | tf_op jit(solution)/shard_map/reduce_scatter | solution.py:85
  215.4 6.3 %fusion = f32[2,6,8,8,8,8]{5,3,4,2,1,0:T(8,128)} fusion(bf16[2,6,8,8,256,1]{4,3,5,2,1,0:T(8,128)(2,1)} %bitcast.78, bf16[2,6,8,8,256]{4,3,2,1,0:T(8,128)(2,1)} %bitcast.77, f32[256]{0:T(256)S(1)} %dynamic_slice.7), kind=kOutput, calls=%fused_computation.11 | convolution fusion | flops 151388160 | bytes 984064 | tf_op jit(solution)/shard_map/qsavr,qscdr->qsacvd/dot_general | solution.py:30
  221.6 4.3 %copy.11 = f32[2,6,8,8,8,8]{2,3,4,0,5,1:T(8,128)S(1)} copy(f32[2,6,8,8,8,8]{5,3,4,2,1,0:T(8,128)} %fusion) | data formatting | bytes 393216 | tf_op jit(solution)/shard_map/qsavr,qscdr->qsacvd/dot_general | solution.py:30
  226.0 13.6 %reduce-scatter.8.cloned.1.call-done = bf16[384,256]{1,0:T(8,128)(2,1)} async-done(((bf16[384,1024]{1,0:T(8,128)(2,1)}), bf16[384,256]{1,0:T(8,128)(2,1)}) %reduce-scatter.8.cloned.1.call-update) | async-done | bytes 196624 | tf_op jit(solution)/shard_map/reduce_scatter | solution.py:79
  239.6 3.5 %bitcast_subtract_fusion = bf16[2,6,8,8,8,8]{3,5,2,0,4,1:T(8,128)(2,1)} fusion(f32[2,6,8,8,8,8]{2,3,4,0,5,1:T(8,128)S(1)} %copy.11, bf16[6,8,8,256,1,1]{3,2,5,4,1,0:T(8,128)(2,1)} %bitcast.79, f32[2,8,8,256,1,1]{3,2,1,0,5,4:T(8,128)S(1)} %bitcast.76), kind=kOutput, calls=%fused_computation.5 | convolution fusion | flops 151142400 | bytes 622592 | tf_op jit(solution)/shard_map/qacr,svdr->qsacvd/dot_general | solution.py:27
  243.0 2.1 copy.12
  245.2 1.7 reshape.286
  247.0 7.4 %copy.17 = bf16[2,6,4096]{0,1,2:T(8,128)(2,1)} copy(bf16[2,6,4096]{2,0,1:T(2,128)(2,1)S(1)} %select_convert_fusion) | data formatting | bytes 196608
  254.4 9.5 %reshape.297 = bf16[4096,12]{1,0:T(8,128)(2,1)} reshape(bf16[4096,6,2]{2,1,0:T(8,128)(2,1)} %bitcast.70) | data formatting | bytes 196608
  263.9 27.0 %reduce-scatter.16.cloned.1.call-done = bf16[1024,12]{1,0:T(8,128)(2,1)} async-done(((bf16[4096,12]{1,0:T(8,128)(2,1)}), bf16[1024,12]{1,0:T(8,128)(2,1)}) %reduce-scatter.16.cloned.1.call-update) | async-done | bytes 24592
  290.9 2.4 reshape.298
  293.3 1.2 copy.18
  294.5 0.6 convert_element_type.152
  (28 shorter events, 1.5 us)
Async XLA Ops:
  6.5 50.8 %all-gather.3.cloned.1.call-start = ((), (), s32[]{:S(2)}) async-start(), calls=%async_computation.5 | async-start | bytes 7077888 | tf_op jit(solution)/shard_map/all_gather | solution.py:48
  7.3 97.4 %all-gather.5.cloned.1.call-start = ((), (), s32[]{:S(2)}) async-start(), calls=%async_computation.6 | async-start | bytes 7077888 | tf_op jit(solution)/shard_map/all_gather | solution.py:51
  8.0 163.2 %reduce-scatter.10.cloned.1.call-start = ((), (), s32[]{:S(2)}) async-start(), calls=%async_computation.8 | async-start | bytes 327680 | tf_op jit(solution)/shard_map/reduce_scatter | solution.py:76
  116.2 62.7 %reduce-scatter.14.cloned.1.call-start = ((), (), s32[]{:S(2)}) async-start(), calls=%async_computation.10 | async-start | bytes 1966080 | tf_op jit(solution)/shard_map/reduce_scatter | solution.py:82
  143.3 72.1 %reduce-scatter.12.cloned.1.call-start = ((), (), s32[]{:S(2)}) async-start(), calls=%async_computation.9 | async-start | bytes 1966080 | tf_op jit(solution)/shard_map/reduce_scatter | solution.py:85
  159.2 80.3 %reduce-scatter.8.cloned.1.call-start = ((), (), s32[]{:S(2)}) async-start(), calls=%async_computation.7 | async-start | bytes 983040 | tf_op jit(solution)/shard_map/reduce_scatter | solution.py:79
  160.1 10.9 %copy-start = (s32[6]{0:T(128)S(1)}, s32[6]{0:T(128)}, u32[]{:S(2)}) copy-start(s32[6]{0:T(128)} %param.13) | copy-start | bytes 76
  160.2 10.9 %copy-start.1 = (s32[2]{0:T(128)S(1)}, s32[2]{0:T(128)}, u32[]{:S(2)}) copy-start(s32[2]{0:T(128)} %param.12) | copy-start | bytes 28
  169.3 121.6 %reduce-scatter.16.cloned.1.call-start = ((), (), s32[]{:S(2)}) async-start(), calls=%async_computation.11 | async-start | bytes 1310720
Sparse Core Ops, SparseCore 0:
  9.2 48.1 all-gather.2
  59.2 45.3 all-gather.4
  116.3 19.9 reduce-scatter.9
  143.4 35.4 reduce-scatter.13
  181.0 34.2 reduce-scatter.11
  217.5 21.9 reduce-scatter.7
  264.0 26.8 reduce-scatter.15
where the time goes:
time: 303 us; the launch traced here: 302 us
  waiting for transfers between devices  177 us (58%)
  matrix products  65.4 us (22%)
  local copies, waits for them, and re-layouts  30.3 us (10%)
  other arithmetic  15.2 us (5%)
  between operations  13.6 us (4%)
    all_gather x1, waiting for transfers between devices, shards(): lax.all_gather(valence_wavefunction, ('vp', 'cp'), axis=0, tiled=True)  48.2 us
    all_gather x1, waiting for transfers between devices, shards(): lax.all_gather(cond_wave, ('vp', 'cp'), axis=0, tiled=True)  43.1 us
    reduce_scatter x1, waiting for transfers between devices, shards(): lax.psum_scatter(cond_part.astype(jnp.bfloat16), 'ga', scatter_dimension=...  36.5 us
    unnamed x8, waiting for transfers between devices  28.5 us
    unnamed x8, local copies, waits for them, and re-layouts  20.5 us
    dot_general x1, matrix products, shards(): jnp.dot(cond_rho, screen_basis, preferred_element_type=jnp.float32)  15.7 us
    dot_general x1, matrix products, shards(): jnp.dot(val_rho, screen_basis, preferred_element_type=jnp.float32)  15.7 us
    reduce_scatter x1, waiting for transfers between devices, shards(): lax.psum_scatter(col_part.astype(jnp.bfloat16), 'ga', scatter_dimension=1...  13.6 us
  transfers between devices with their start and end apart: 7, of which 6 were waited for; matrix products, arithmetic and copies ran while one was open for 23% of the time, Pallas kernels for 0%

commit v1 on v0

--- a/solution.py
+++ b/solution.py
@@ -45,7 +45,13 @@
         (pair_tiles % NCT)[:, None] * TC + jnp.arange(TC, dtype=jnp.int32)[None, :]
     ).reshape(-1)
     picked_val = select_bands(
-        val_wanted, lax.all_gather(valence_wavefunction, ("vp", "cp"), axis=0, tiled=True)
+        val_wanted,
+        jnp.concatenate(
+            lax.all_to_all(
+                jnp.stack([valence_wavefunction] * lax.axis_size(("vp", "cp"))), ("vp", "cp"), 0, 0
+            ),
+            axis=0,
+        ),
     )
     picked_cond = select_bands(
         conduction_wanted, lax.all_gather(cond_wave, ("vp", "cp"), axis=0, tiled=True)

time: 303 us -> 316 us (1.043)
  starting transfers between devices: 0.65 us -> 5.94 us
  local copies, waits for them, and re-layouts: 30.3 us -> 34.9 us
    all_to_all x0 -> x1, waiting for transfers between devices: none -> 96.7 us  [shards(): lax.all_to_all(jnp.stack([valence_wavefunction] * lax.axis_size(('vp', 'c...]
    all_gather x1 -> x0, waiting for transfers between devices: 48.2 us -> none  [shards(): lax.all_gather(valence_wavefunction, ('vp', 'cp'), axis=0, tiled=True)]
    all_gather x1, waiting for transfers between devices: 43.1 us -> 0.01 us  [shards(): lax.all_gather(cond_wave, ('vp', 'cp'), axis=0, tiled=True)]
    all_to_all x0 -> x1, starting transfers between devices: none -> 5.33 us  [shards(): lax.all_to_all(jnp.stack([valence_wavefunction] * lax.axis_size(('vp', 'c...]
    another operation x0 -> x1, local copies, waits for them, and re-layouts: none -> 4.55 us  [shards(): jnp.stack([valence_wavefunction] * lax.axis_size(('vp', 'cp')))]
    unnamed x8 -> x7, waiting for transfers between devices: 28.5 us -> 27.7 us
  transfers between devices with their start and end apart: 7 -> 7, of which waited for: 6 -> 5; matrix products, arithmetic and copies ran while one was open for 23% -> 24% of each run, Pallas kernels for 0% -> 0%
where the time goes in v1:
time: 316 us; the launch traced here: 315 us
  waiting for transfers between devices  180 us (57%)
  matrix products  65.6 us (21%)
  local copies, waits for them, and re-layouts  34.9 us (11%)
  other arithmetic  14.5 us (5%)
  between operations  13.6 us (4%)
  starting transfers between devices  5.94 us (2%)
    all_to_all x1, waiting for transfers between devices, shards(): lax.all_to_all(jnp.stack([valence_wavefunction] * lax.axis_size(('vp', 'c...  96.7 us
    reduce_scatter x1, waiting for transfers between devices, shards(): lax.psum_scatter(cond_part.astype(jnp.bfloat16), 'ga', scatter_dimension=...  36.5 us
    unnamed x7, waiting for transfers between devices  27.7 us
    unnamed x8, local copies, waits for them, and re-layouts  20.5 us
    dot_general x1, matrix products, shards(): jnp.dot(val_rho, screen_basis, preferred_element_type=jnp.float32)  15.7 us
    dot_general x1, matrix products, shards(): jnp.dot(cond_rho, screen_basis, preferred_element_type=jnp.float32)  15.7 us
    reduce_scatter x1, waiting for transfers between devices, shards(): lax.psum_scatter(col_part.astype(jnp.bfloat16), 'ga', scatter_dimension=1...  13.5 us
    convert_element_type x4, other arithmetic, outer_rows(): return product.astype(jnp.bfloat16)  12.4 us
  transfers between devices with their start and end apart: 7, of which 5 were waited for; matrix products, arithmetic and copies ran while one was open for 24% of the time, Pallas kernels for 0%

profile of v1, /device:TPU:0, one launch (start us, length us, event | category | flops | bytes accessed | tf_op | source)
XLA Modules:
  0.0 315.0 jit_solution(9522621604737508078)
XLA Ops:
  6.5 0.7 all-gather.2.cloned.1.call-update
  7.3 4.5 %stack.2 = bf16[8,64,6144]{2,1,0:T(8,128)(2,1)} broadcast(bf16[64,6144]{1,0:T(8,128)(2,1)} %param.7), dimensions={1,2} | broadcast | bytes 7077888 | tf_op jit(solution)/shard_map/stack | solution.py:51
  11.8 5.3 %all-to-all-start = ((bf16[8,64,6144]{2,1,0:T(8,128)(2,1)}), bf16[8,64,6144]{2,1,0:T(8,128)(2,1)}, u32[]{:S(2)}, u32[]{:S(2)}) async-start(bf16[8,64,6144]{2,1,0:T(8,128)(2,1)} %stack.2), calls=%async_computation | async-start | bytes 12582912 | tf_op jit(solution)/shard_map/all_to_all | solution.py:50
  17.6 96.7 %all-to-all-done = bf16[8,64,6144]{2,1,0:T(8,128)(2,1)} async-done(((bf16[8,64,6144]{2,1,0:T(8,128)(2,1)}), bf16[8,64,6144]{2,1,0:T(8,128)(2,1)}, u32[]{:S(2)}, u32[]{:S(2)}) %all-to-all-start) | async-done | bytes 6291488 | tf_op jit(solution)/shard_map/all_to_all | solution.py:50
  114.3 4.0 %convolution_convert_fusion.1 = bf16[64,6144]{1,0:T(8,128)(2,1)S(1)} fusion(bf16[512,6144]{1,0:T(8,128)(2,1)} %bitcast, s32[64]{0:T(128)S(1)} %add.72), kind=kOutput, calls=%fused_computation.4 | convolution fusion | flops 403079168 | bytes 7078144 | tf_op jit(solution)/shard_map/dot_general | solution.py:15
  118.4 5.7 %multiply_convert_fusion = bf16[2,6,8,8,6144]{4,3,2,1,0:T(8,128)(2,1)} fusion(f32[6,8,6144]{2,1,0:T(8,128)S(1)} %fusion.3, f32[2,8,6144]{2,1,0:T(8,128)S(1)} %fusion.6), kind=kLoop, calls=%fused_computation | loop fusion | flops 9437184 | bytes 11010048 | tf_op jit(solution)/shard_map/convert_element_type | solution.py:23
  124.1 4.0 %convolution_convert_fusion = bf16[64,6144]{1,0:T(8,128)(2,1)S(1)} fusion(bf16[512,6144]{1,0:T(8,128)(2,1)} %all-gather.2.cloned.1.call-done, s32[64]{0:T(128)S(1)} %add.77), kind=kOutput, calls=%fused_computation.3 | convolution fusion | flops 403079168 | bytes 7078144 | tf_op jit(solution)/shard_map/dot_general | solution.py:15
  128.2 0.2 multiply_convert_fusion.3
  128.4 7.1 %convolution_convert_fusion.5 = bf16[128,1024]{1,0:T(8,128)(2,1)} fusion(bf16[128,6144]{1,0:T(8,128)(2,1)S(1)} %bitcast.72, bf16[6144,1024]{1,0:T(8,128)(2,1)} %param.9), kind=kOutput, calls=%fused_computation.10 | convolution fusion | flops 1610743808 | bytes 14417920 | tf_op jit(solution)/shard_map/dot_general | solution.py:73
  135.6 15.7 %convolution_convert_fusion.2 = bf16[768,1024]{1,0:T(8,128)(2,1)} fusion(bf16[768,6144]{1,0:T(8,128)(2,1)} %bitcast.73, bf16[6144,1024]{1,0:T(8,128)(2,1)} %param.9), kind=kOutput, calls=%fused_computation.7 | convolution fusion | flops 9664462848 | bytes 23592960 | tf_op jit(solution)/shard_map/dot_general | solution.py:75
  151.7 5.7 %multiply_convert_fusion.1 = bf16[2,6,8,8,6144]{4,3,2,1,0:T(8,128)(2,1)} fusion(f32[6,8,6144]{2,1,0:T(8,128)S(1)} %fusion.2, f32[2,8,6144]{2,1,0:T(8,128)S(1)} %fusion.5), kind=kLoop, calls=%fused_computation.1 | loop fusion | flops 9437184 | bytes 11010048 | tf_op jit(solution)/shard_map/convert_element_type | solution.py:23
  157.3 15.7 %convolution_convert_fusion.3 = bf16[768,1024]{1,0:T(8,128)(2,1)} fusion(bf16[768,6144]{1,0:T(8,128)(2,1)} %bitcast.74, bf16[6144,1024]{1,0:T(8,128)(2,1)} %param.9), kind=kOutput, calls=%fused_computation.8 | convolution fusion | flops 9664462848 | bytes 23592960 | tf_op jit(solution)/shard_map/dot_general | solution.py:76
  173.0 0.8 multiply_convert_fusion.2
  173.9 9.1 %convolution_convert_fusion.4 = bf16[384,1024]{1,0:T(8,128)(2,1)} fusion(bf16[384,6144]{1,0:T(8,128)(2,1)S(1)} %bitcast.76, bf16[6144,1024]{1,0:T(8,128)(2,1)} %param.9), kind=kOutput, calls=%fused_computation.9 | convolution fusion | flops 4832231424 | bytes 18087936 | tf_op jit(solution)/shard_map/dot_general | solution.py:74
  183.0 0.3 reduce-scatter.16.cloned.1.call-start
  183.3 0.8 dynamic_slice.7
  184.1 0.8 dynamic_slice.6
  184.9 0.9 convert_multiply_fusion.2
  185.8 6.1 %reduce-scatter.14.cloned.1.call-done = bf16[768,256]{1,0:T(8,128)(2,1)} async-done(((bf16[768,1024]{1,0:T(8,128)(2,1)}), bf16[768,256]{1,0:T(8,128)(2,1)}) %reduce-scatter.14.cloned.1.call-update) | async-done | bytes 393232 | tf_op jit(solution)/shard_map/reduce_scatter | solution.py:88
  191.9 36.5 %reduce-scatter.12.cloned.1.call-done = bf16[768,256]{1,0:T(8,128)(2,1)} async-done(((bf16[768,1024]{1,0:T(8,128)(2,1)}), bf16[768,256]{1,0:T(8,128)(2,1)}) %reduce-scatter.12.cloned.1.call-update) | async-done | bytes 393232 | tf_op jit(solution)/shard_map/reduce_scatter | solution.py:91
  228.3 6.3 %fusion = f32[2,6,8,8,8,8]{5,3,4,2,1,0:T(8,128)} fusion(bf16[2,6,8,8,256,1]{4,3,5,2,1,0:T(8,128)(2,1)} %bitcast.79, bf16[2,6,8,8,256]{4,3,2,1,0:T(8,128)(2,1)} %bitcast.78, f32[256]{0:T(256)S(1)} %dynamic_slice.7), kind=kOutput, calls=%fused_computation.11 | convolution fusion | flops 151388160 | bytes 984064 | tf_op jit(solution)/shard_map/qsavr,qscdr->qsacvd/dot_general | solution.py:30
  234.7 4.3 %copy.11 = f32[2,6,8,8,8,8]{2,3,4,0,5,1:T(8,128)S(1)} copy(f32[2,6,8,8,8,8]{5,3,4,2,1,0:T(8,128)} %fusion) | data formatting | bytes 393216 | tf_op jit(solution)/shard_map/qsavr,qscdr->qsacvd/dot_general | solution.py:30
  239.0 13.5 %reduce-scatter.8.cloned.1.call-done = bf16[384,256]{1,0:T(8,128)(2,1)} async-done(((bf16[384,1024]{1,0:T(8,128)(2,1)}), bf16[384,256]{1,0:T(8,128)(2,1)}) %reduce-scatter.8.cloned.1.call-update) | async-done | bytes 196624 | tf_op jit(solution)/shard_map/reduce_scatter | solution.py:85
  252.5 3.6 %bitcast_subtract_fusion = bf16[2,6,8,8,8,8]{3,5,2,0,4,1:T(8,128)(2,1)} fusion(f32[2,6,8,8,8,8]{2,3,4,0,5,1:T(8,128)S(1)} %copy.11, bf16[6,8,8,256,1,1]{3,2,5,4,1,0:T(8,128)(2,1)} %bitcast.80, f32[2,8,8,256,1,1]{3,2,1,0,5,4:T(8,128)S(1)} %bitcast.77), kind=kOutput, calls=%fused_computation.5 | convolution fusion | flops 151142400 | bytes 622592 | tf_op jit(solution)/shard_map/qacr,svdr->qsacvd/dot_general | solution.py:27
  256.1 2.1 copy.12
  258.2 1.7 reshape.292
  260.0 7.4 %copy.17 = bf16[2,6,4096]{0,1,2:T(8,128)(2,1)} copy(bf16[2,6,4096]{2,0,1:T(2,128)(2,1)S(1)} %select_convert_fusion) | data formatting | bytes 196608
  267.4 9.5 %reshape.303 = bf16[4096,12]{1,0:T(8,128)(2,1)} reshape(bf16[4096,6,2]{2,1,0:T(8,128)(2,1)} %bitcast.71) | data formatting | bytes 196608
  277.0 26.9 %reduce-scatter.16.cloned.1.call-done = bf16[1024,12]{1,0:T(8,128)(2,1)} async-done(((bf16[4096,12]{1,0:T(8,128)(2,1)}), bf16[1024,12]{1,0:T(8,128)(2,1)}) %reduce-scatter.16.cloned.1.call-update) | async-done | bytes 24592
  303.9 2.4 reshape.304
  306.3 1.2 copy.18
  307.5 0.6 convert_element_type.152
  (28 shorter events, 1.3 us)
Async XLA Ops:
  6.5 117.5 %all-gather.2.cloned.1.call-start = ((), (), s32[]{:S(2)}) async-start(), calls=%async_computation.6 | async-start | bytes 7077888 | tf_op jit(solution)/shard_map/all_gather | solution.py:57
  11.8 5.4 %copy-start = (s32[6]{0:T(128)S(1)}, s32[6]{0:T(128)}, u32[]{:S(2)}) copy-start(s32[6]{0:T(128)} %param.13) | copy-start | bytes 76
  11.8 5.4 %copy-start.1 = (s32[2]{0:T(128)S(1)}, s32[2]{0:T(128)}, u32[]{:S(2)}) copy-start(s32[2]{0:T(128)} %param.12) | copy-start | bytes 28
  11.8 102.5 %all-to-all-start = ((bf16[8,64,6144]{2,1,0:T(8,128)(2,1)}), bf16[8,64,6144]{2,1,0:T(8,128)(2,1)}, u32[]{:S(2)}, u32[]{:S(2)}) async-start(bf16[8,64,6144]{2,1,0:T(8,128)(2,1)} %stack.2), calls=%async_computation | async-start | bytes 12582912 | tf_op jit(solution)/shard_map/all_to_all | solution.py:50
  17.1 167.8 %reduce-scatter.10.cloned.1.call-start = ((), (), s32[]{:S(2)}) async-start(), calls=%async_computation.8 | async-start | bytes 327680 | tf_op jit(solution)/shard_map/reduce_scatter | solution.py:82
  135.5 56.3 %reduce-scatter.14.cloned.1.call-start = ((), (), s32[]{:S(2)}) async-start(), calls=%async_computation.10 | async-start | bytes 1966080 | tf_op jit(solution)/shard_map/reduce_scatter | solution.py:88
  151.3 77.0 %reduce-scatter.12.cloned.1.call-start = ((), (), s32[]{:S(2)}) async-start(), calls=%async_computation.9 | async-start | bytes 1966080 | tf_op jit(solution)/shard_map/reduce_scatter | solution.py:91
  173.0 79.5 %reduce-scatter.8.cloned.1.call-start = ((), (), s32[]{:S(2)}) async-start(), calls=%async_computation.7 | async-start | bytes 983040 | tf_op jit(solution)/shard_map/reduce_scatter | solution.py:85
  183.0 120.8 %reduce-scatter.16.cloned.1.call-start = ((), (), s32[]{:S(2)}) async-start(), calls=%async_computation.11 | async-start | bytes 1310720
Sparse Core Ops, SparseCore 0:
  9.2 89.2 all-gather.1
  135.7 20.1 reduce-scatter.9
  158.2 33.6 reduce-scatter.13
  194.0 34.2 reduce-scatter.11
  230.5 21.9 reduce-scatter.7
  277.1 26.7 reduce-scatter.15
